TPU v7x, 128 devices: a whole 4x4x4 slice. The times are simulated.
128 devices in a mesh: comp: 4 (over y), lat: 4 (over z), lon: 8 (over x, core).
Axes of the slice: x: 4, y: 4, z: 4, core: 2. Of those that a mesh axis runs over, the one named last changes fastest.
Arguments:
- state: float32 [2048, 1024, 128], P(('comp', 'lat'), 'lon'), may hold values from -6 to 6
- land_mask: int32 [2048, 1024], P(('comp', 'lat'), 'lon'), may hold values 0 or 1
- intersection_list: int32 [2048, 8, 2, 3], P(('comp', 'lat'), 'lon'), may hold values from 0 to 127, as said below
- mix_atm: float32 [128, 128], replicated, may hold values from -0.5 to 0.5
- mix_ocn: float32 [128, 128], replicated, may hold values from -0.5 to 0.5
- flux_map: float32 [128, 8], replicated, may hold values from -0.5 to 0.5
- ocean_map: float32 [8, 128], replicated, may hold values from -2 to 2
- regrid_weights: bfloat16 [32, 128, 128], replicated, may hold values from -0.25 to 0.25
Outputs:
- state_out: float32 [2048, 1024, 128], P(('comp', 'lat'), 'lon')
- surface_out: float32 [2048, 1024], P(('comp', 'lat'), 'lon')
Inputs may be any that keep to these rules, and one draw needn't show every extreme that they name: `intersection_list`: entry 0 is an ocean tile lat * 8 + lon, entry 1 a row of that tile below 128, entry 2 a weight block below 32. With t the tile lat * 8 + lon of the list's own rows and r = min(4, 8), the entries of one tile name exactly the 2 r tiles (t + a * 8 + b - (r - 1) // 2) mod (4 * 8) for a in 0, 1 and b in 0 to r - 1, each by exactly 32 entries.
All inputs are finite; a program needn't handle non-finite values. No bound on the sum of `land_mask` on one device may be relied on, other than what follows from the above.
Results may differ from a plain program's by a relative error of at most 0.0012.
Values may be sent and summed in bfloat16 or wider, within the bound.
A program may use at most 192 MiB of HBM per device.

v0:
```python
import jax
import jax.numpy as jnp
from jax import lax
from jax.sharding import PartitionSpec as P

SMOOTHING = 0.2
PHYSICS = 0.5
HIGHEST = lax.Precision.HIGHEST


def with_halo(shard, sides, width, wrap):
    for axis, dim in sides:
        size, length = (lax.axis_size(axis), shard.shape[dim])
        up = [(i, (i + 1) % size) for i in range(size if wrap else size - 1)]
        down = [(j, i) for i, j in up]
        last = lax.slice_in_dim(shard, length - width, length, axis=dim)
        leading = lax.slice_in_dim(shard, 0, width, axis=dim)
        before = lax.ppermute(last, axis, up)
        after = lax.ppermute(leading, axis, down)
        shard = jnp.concatenate([before, shard, after], axis=dim)
    return shard


def from_behind(value, axis, steps):
    count = lax.axis_size(axis)
    pairs = [(source, (source + steps) % count) for source in range(count)]
    return lax.ppermute(value, axis, pairs)


def shortened(shard):
    return jax.tree.map(lambda a: a.astype(jnp.bfloat16) if a.dtype == jnp.float32 else a, shard)


def column_physics(values, mixing):
    return jnp.tanh(jnp.einsum("rck,kj->rcj", values, mixing, precision=HIGHEST))


def earlier_same(owners, usable):
    positions = jnp.arange(owners.shape[0], dtype=jnp.int32)
    before = (
        (owners[None, :] == owners[:, None])
        & (positions[None, :] < positions[:, None])
        & usable[None, :]
    )
    return jnp.sum(before.astype(jnp.int32), axis=1)


def pack_rows(blocks, owners, labels, usable, slots_each, owner_total):
    ranks = earlier_same(owners, usable)
    target_slot = owners * slots_each + ranks
    slot_ids = jnp.arange(owner_total * slots_each, dtype=jnp.int32)
    placing = (slot_ids[:, None] == target_slot[None, :]) & usable[None, :]
    packed = jnp.dot(
        placing.astype(jnp.bfloat16), blocks, preferred_element_type=jnp.float32
    ).astype(jnp.bfloat16)
    placed_labels = jnp.sum(jnp.where(placing, labels[None, :] + 1, 0), axis=1) - 1
    return (
        packed.reshape(owner_total, slots_each, blocks.shape[1]),
        placed_labels.reshape(owner_total, slots_each),
    )


def local(
    state, land_mask, intersection_list, mix_atm, mix_ocn, flux_map, ocean_map, regrid_weights
):
    tile_rows, block_len, levels = state.shape
    flux_count = flux_map.shape[1]
    weight_count = regrid_weights.shape[0]
    intersections = intersection_list.shape[2]
    comp_count = lax.axis_size("comp")
    lat_count = lax.axis_size("lat")
    lon_count = lax.axis_size("lon")
    tile_count = lat_count * lon_count
    reach = min(4, lon_count)
    neighbour_count = 2 * reach
    capacity = intersections * tile_rows // neighbour_count
    quarter = capacity // comp_count
    width = flux_count * block_len
    comp_index = lax.axis_index("comp")
    tile_index = lax.axis_index("lat") * lon_count + lax.axis_index("lon")
    band = comp_index * lat_count + lax.axis_index("lat")
    ocean_band = (comp_count - 1) * lat_count
    ocean_side = comp_index == comp_count - 1
    lower_valid = (band > 0) & ((band - 1 >= ocean_band) == (band >= ocean_band))
    upper_valid = (band < comp_count * lat_count - 1) & (
        (band + 1 >= ocean_band) == (band >= ocean_band)
    )
    sea_cells = land_mask == 1
    current = state
    flux_total = jnp.zeros((flux_count, tile_rows, block_len), jnp.float32)
    ocean_spread = None
    for substep in range(2):
        padded = with_halo(current.astype(jnp.bfloat16), ((("comp", "lat"), 0),), 1, False).astype(
            current.dtype
        )
        below = jnp.concatenate([jnp.where(lower_valid, padded[:1], 0.0), current[:-1]], axis=0)
        above = jnp.concatenate([current[1:], jnp.where(upper_valid, padded[-1:], 0.0)], axis=0)
        sides = with_halo(current, (("lon", 1),), 1, True)
        spread = below + above + sides[:, :-2] + sides[:, 2:] - 4.0 * current
        if substep == 0:
            ocean_spread = spread

        def advance(operands):
            values, spread_now, total = operands
            smooth = values + SMOOTHING * spread_now
            moved = smooth + PHYSICS * column_physics(smooth, mix_atm)
            return (moved, total + jnp.einsum("rck,kf->frc", moved, flux_map, precision=HIGHEST))

        def resting(operands):
            return (operands[0], operands[2])

        current, flux_total = lax.cond(ocean_side, resting, advance, (current, spread, flux_total))
    flux_sent = jnp.where(sea_cells[None], 0.5 * flux_total, 0.0).astype(jnp.bfloat16)
    entry_list = intersection_list.reshape(tile_rows * intersections, 3)
    owners = entry_list[:, 0]
    targets = entry_list[:, 1]
    weight_ids = entry_list[:, 2]
    labels = weight_ids * tile_rows + targets
    entry_blocks = jnp.repeat(flux_sent.transpose(1, 0, 2), intersections, axis=0).reshape(
        tile_rows * intersections, width
    )
    sending = jnp.broadcast_to(jnp.logical_not(ocean_side), owners.shape)
    offsets = [
        (n // reach * lon_count + n % reach - (reach - 1) // 2) % tile_count
        for n in range(neighbour_count)
    ]
    offset_table = jnp.array(offsets, jnp.int32)
    distance = (owners - tile_index + tile_count) % tile_count
    neighbour_ids = jnp.sum(
        jnp.where(
            distance[:, None] == offset_table[None, :],
            jnp.arange(neighbour_count, dtype=jnp.int32)[None, :],
            0,
        ),
        axis=1,
    )
    packed, packed_labels = pack_rows(
        entry_blocks, neighbour_ids, labels, sending, capacity, neighbour_count
    )
    moved_blocks = []
    moved_labels = []
    for neighbour in range(neighbour_count):
        if offsets[neighbour] == 0:
            one_blocks, one_labels = (packed[neighbour], packed_labels[neighbour])
        else:
            one_blocks, one_labels = from_behind(
                (packed[neighbour], packed_labels[neighbour]), ("lat", "lon"), offsets[neighbour]
            )
        moved_blocks.append(one_blocks)
        moved_labels.append(one_labels)
    stacked_blocks = jnp.stack(moved_blocks).reshape(neighbour_count, comp_count, quarter, width)
    stacked_labels = jnp.stack(moved_labels).reshape(neighbour_count, comp_count, quarter)
    arrived, arrived_labels = (
        lax.all_to_all(stacked_blocks, "comp", split_axis=1, concat_axis=1, tiled=True),
        lax.all_to_all(
            shortened(stacked_labels), "comp", split_axis=1, concat_axis=1, tiled=True
        ).astype(stacked_labels.dtype),
    )
    weights_wide = regrid_weights.astype(jnp.float32)
    label_ids = jnp.arange(weight_count * tile_rows, dtype=jnp.int32)
    flat_labels = arrived_labels.reshape(-1)
    selector = (flat_labels[:, None] == label_ids[None, :]).astype(jnp.bfloat16)
    binned = lax.dot_general(
        selector,
        arrived.reshape(flat_labels.shape[0], width),
        (((0,), (0,)), ((), ())),
        preferred_element_type=jnp.float32,
    )
    binned = binned.reshape(weight_count, tile_rows, flux_count, block_len)
    partial_forcing = jnp.einsum("wdfa,wab->fdb", binned, weights_wide, precision=HIGHEST)
    forcing = lax.psum(partial_forcing, "comp")

    def ocean_step(values):
        smooth = values + SMOOTHING * ocean_spread
        moved = (
            smooth
            + jnp.einsum("frc,fk->rck", forcing, ocean_map, precision=HIGHEST)
            + PHYSICS * column_physics(smooth, mix_ocn)
        )
        return jnp.where(sea_cells[:, :, None], moved, values)

    def unchanged(values):
        return values

    final_state = lax.cond(ocean_side, ocean_step, unchanged, current)
    surface = final_state[:, :, 0]
    everything = lax.all_gather(surface, ("comp", "lat", "lon"), axis=0, tiled=True)
    ocean_surface = everything[(comp_count - 1) * tile_count * tile_rows :]
    picked = jnp.take(ocean_surface, owners * tile_rows + targets, axis=0)
    images = jnp.einsum("eb,wab->ewa", picked, weights_wide, precision=HIGHEST)
    which_block = weight_ids[:, None] == jnp.arange(weight_count, dtype=jnp.int32)[None, :]
    chosen = jnp.sum(jnp.where(which_block[:, :, None], images, 0.0), axis=1)
    returned = chosen.reshape(tile_rows, intersections, block_len).sum(axis=1)
    surface_out = jnp.where(ocean_side, surface, jnp.where(sea_cells, returned, surface))
    return (final_state, surface_out)


def solution(mesh):
    placed = (
        P(("comp", "lat"), "lon", None),
        P(("comp", "lat"), "lon"),
        P(("comp", "lat"), "lon", None, None),
        P(),
        P(),
        P(),
        P(),
        P(),
    )
    return jax.shard_map(
        local,
        mesh=mesh,
        in_specs=placed,
        out_specs=(P(("comp", "lat"), "lon", None), P(("comp", "lat"), "lon")),
        check_vma=False,
    )
```

profile of v0, /device:TPU:1, one launch (start us, length us, event | category | flops | bytes accessed | tf_op | source)
XLA Modules:
  0.0 446.0 jit_solution(6722791696484953840)
XLA Ops:
  7.2 8.0 %copy.117 = f32[128,128,128]{2,1,0:T(8,128)} copy(f32[128,128,128]{2,1,0:T(8,128)} %param.15) | data formatting | bytes 16777216
  15.2 4.4 convert_element_type.30
  19.6 1.9 copy-done.1
  21.5 4.4 collective-permute-start
  25.9 1.3 collective-permute-start.1
  27.2 1.3 fusion.42
  28.5 2.1 collective-permute-start.2
  31.4 1.9 collective-permute-start.8
  33.3 10.9 %fusion.41 = (f32[127,128,128]{2,1,0:T(8,128)}, f32[127,128,128]{2,1,0:T(8,128)}) fusion(f32[128,128,128]{2,1,0:T(8,128)} %copy.117), kind=kLoop, calls=%fused_computation.103 | loop fusion | bytes 33292288 | tf_op jit(solution)/shard_map/slice | solution.py:97
  44.5 4.7 %collective-permute-done.9 = s32[32]{0:T(128)S(1)} collective-permute-done((s32[32]{0:T(128)S(1)}, s32[32]{0:T(128)S(1)}, u32[]{:S(2)}, u32[]{:S(2)}) %collective-permute-start.9) | collective-permute-done | bytes 160 | tf_op jit(solution)/shard_map/ppermute | solution.py:27
  49.3 5.6 %collective-permute-done.10 = s32[32]{0:T(128)S(1)} collective-permute-done((s32[32]{0:T(128)S(1)}, s32[32]{0:T(128)S(1)}, u32[]{:S(2)}, u32[]{:S(2)}) %collective-permute-start.10) | collective-permute-done | bytes 160 | tf_op jit(solution)/shard_map/ppermute | solution.py:27
  54.9 2.5 collective-permute-start.11
  57.4 2.5 collective-permute-done.11
  60.0 0.4 collective-permute-start.12
  60.5 5.4 %collective-permute-done.12 = s32[32]{0:T(128)S(1)} collective-permute-done((s32[32]{0:T(128)S(1)}, s32[32]{0:T(128)S(1)}, u32[]{:S(2)}, u32[]{:S(2)}) %collective-permute-start.12) | collective-permute-done | bytes 160 | tf_op jit(solution)/shard_map/ppermute | solution.py:27
  66.0 5.2 %collective-permute-done.13 = s32[32]{0:T(128)S(1)} collective-permute-done((s32[32]{0:T(128)S(1)}, s32[32]{0:T(128)S(1)}, u32[]{:S(2)}, u32[]{:S(2)}) %collective-permute-start.13) | collective-permute-done | bytes 160 | tf_op jit(solution)/shard_map/ppermute | solution.py:27
  71.3 5.9 %collective-permute-done.14 = s32[32]{0:T(128)S(1)} collective-permute-done((s32[32]{0:T(128)S(1)}, s32[32]{0:T(128)S(1)}, u32[]{:S(2)}, u32[]{:S(2)}) %collective-permute-start.14) | collective-permute-done | bytes 160 | tf_op jit(solution)/shard_map/ppermute | solution.py:27
  77.4 18.3 %fusion.15 = f32[128,128,128]{2,1,0:T(8,128)} fusion(f32[128,1,128]{2,1,0:T(1,128)S(1)} %collective-permute-done.3, f32[128,128,128]{2,1,0:T(8,128)} %copy.117, f32[128,1,128]{2,1,0:T(1,128)S(1)} %collective-permute-done.2, f32[127,128,128]{2,1,0:T(8,128)} %get-tuple-element.139, f32[1,128,128]{2,1,0:T(8,128)S(1)} %get-tuple-element.145, ...), kind=kLoop, calls=%fused_computation.27 | loop fusion | flops 18874368 | bytes 33685504 | tf_op jit(solution)/shard_map/sub | solution.py:99
  95.7 27.4 %conditional.3 = (f32[128,128,128]{2,1,0:T(8,128)}, f32[8,128,128]{2,0,1:T(8,128)S(1)}) conditional(s32[]{:T(128)} %convert_element_type.29, (f32[128,128,128]{2,1,0:T(8,128)}, f32[128,128,128]{2,1,0:T(8,128)}, f32[128,128]{1,0:T(8,128)S(1)}, f32[128,8]{0,1:T(8,128)S(1)}) %tuple.90, f32[128,128,128]{2,1,0:T(8,128)} %copy.117), branch_computations={%region_0.1_spmd, %region_1.2_spmd} | conditional | flops 3435134976 | bytes 50925584 | solution.py:112
  95.9 3.4 copy.115
  99.3 14.4 %multiply_add_fusion = f32[128,128,128]{2,1,0:T(8,128)} fusion(f32[128,128,128]{2,1,0:T(8,128)S(1)} %copy.115, f32[128,128,128]{2,1,0:T(8,128)} %get-tuple-element.62, f32[128,128]{1,0:T(8,128)S(1)} %get-tuple-element.63), kind=kOutput, calls=%fused_computation.1 | convolution fusion | flops 3233808384 | bytes 25231360 | tf_op jit(solution)/shard_map/cond/branch_0_fun/rck,kj->rcj/dot_general | solution.py:35
  113.7 9.4 %convolution_bitcast_fusion = f32[8,128,128]{2,0,1:T(8,128)S(1)} fusion(f32[128,128,128]{2,1,0:T(8,128)} %multiply_add_fusion, f32[128,8]{0,1:T(8,128)S(1)} %get-tuple-element.64), kind=kOutput, calls=%fused_computation.3 | convolution fusion | flops 201326592 | bytes 8916992 | tf_op jit(solution)/shard_map/cond/branch_0_fun/rck,kf->frc/dot_general | solution.py:107
  123.1 4.4 convert_element_type.32
  127.5 6.7 %fusion.40 = (f32[127,128,128]{2,1,0:T(8,128)S(1)}, f32[127,128,128]{2,1,0:T(8,128)S(1)}) fusion(f32[128,128,128]{2,1,0:T(8,128)} %get-tuple-element.86), kind=kLoop, calls=%fused_computation.102 | loop fusion | bytes 33292288 | tf_op jit(solution)/shard_map/slice | solution.py:97
  134.3 3.9 collective-permute-start.4
  138.1 1.3 collective-permute-start.5
  139.4 1.9 fusion.39
  141.4 2.6 collective-permute-start.6
  144.0 1.9 collective-permute-start.7
  146.0 6.9 %pad_maximum_fusion.4 = (f32[128,128,128]{2,1,0:T(8,128)}, f32[128,128,128]{2,1,0:T(8,128)}) fusion(f32[127,128,128]{2,1,0:T(8,128)S(1)} %get-tuple-element.137, f32[1,128,128]{2,1,0:T(8,128)S(1)} %get-tuple-element.143, f32[1,128,128]{2,1,0:T(8,128)S(1)} %get-tuple-element.142, f32[127,128,128]{2,1,0:T(8,128)S(1)} %get-tuple-element.136), kind=kLoop, calls=%fused_computation.31 | loop fusion | flops 4194304 | bytes 33554432 | tf_op jit(solution)/shard_map/concatenate | solution.py:96
  152.8 12.6 %pad_maximum_fusion.1 = (f32[128,129,128]{2,1,0:T(8,128)}, f32[128,129,128]{2,1,0:T(8,128)}) fusion(f32[128,1,128]{2,1,0:T(1,128)} %collective-permute-done.7, f32[128,128,128]{2,1,0:T(8,128)} %get-tuple-element.86, f32[128,1,128]{2,1,0:T(1,128)} %collective-permute-done.6), kind=kLoop, calls=%fused_computation.24 | loop fusion | flops 4227072 | bytes 25427968 | tf_op jit(solution)/shard_map/concatenate | solution.py:20
  165.4 4.3 broadcast.111
  169.8 58.3 %conditional.4 = ((f32[128,128,128]{2,1,0:T(8,128)}, f32[8,128,128]{2,0,1:T(8,128)S(1)})) conditional(s32[]{:T(128)} %convert_element_type.29, (f32[128,128,128]{2,1,0:T(8,128)}, f32[128,128,128]{2,1,0:T(8,128)}, f32[128,129,128]{2,1,0:T(8,128)}, f32[128,129,128]{2,1,0:T(8,128)}, f32[128,128,128]{2,1,0:T(8,128)}, ...), branch_computations={%region_2.3_spmd, %region_3.4_spmd} | conditional | flops 3456237568 | bytes 135335968 | solution.py:112
  169.9 7.8 %copy.116 = f32[128,128,128]{2,1,0:T(8,128)} copy(f32[128,128,128]{2,1,0:T(8,128)} %get-tuple-element.65) | data formatting | bytes 16777216 | tf_op jit(solution)/shard_map/cond
  177.7 40.9 %multiply_add_fusion.3 = f32[128,128,128]{2,1,0:T(8,128)} fusion(f32[128,128,128]{2,1,0:T(8,128)} %copy.116, f32[128,128,128]{2,1,0:T(8,128)} %get-tuple-element.70, f32[128,129,128]{2,1,0:T(8,128)} %get-tuple-element.69, f32[128,129,128]{2,1,0:T(8,128)} %get-tuple-element.68, f32[128,128,128]{2,1,0:T(8,128)} %get-tuple-element.66, ...), kind=kOutput, calls=%fused_computation.7 | convolution fusion | flops 3254779904 | bytes 109117440 | tf_op jit(solution)/shard_map/cond/branch_0_fun/rck,kj->rcj/dot_general | solution.py:35
  218.6 9.4 %fusion.3 = f32[8,128,128]{2,0,1:T(8,128)S(1)} fusion(f32[8,128,128]{2,0,1:T(8,128)S(1)} %get-tuple-element.72, f32[128,128,128]{2,1,0:T(8,128)} %multiply_add_fusion.3, f32[128,8]{0,1:T(8,128)S(1)} %get-tuple-element.73), kind=kOutput, calls=%fused_computation.10 | convolution fusion | flops 201457664 | bytes 9441280 | tf_op jit(solution)/shard_map/cond/branch_0_fun/rck,kf->frc/dot_general | solution.py:107
  228.6 3.0 collective-permute-start.15
  231.6 0.6 copy.61
  232.2 9.5 %all-to-all-start = ((s32[8,4,8]{2,0,1:T(8,128)}), s32[8,4,8]{2,0,1:T(8,128)S(1)}, u32[]{:S(2)}, u32[]{:S(2)}) async-start(s32[8,4,8]{2,0,1:T(8,128)} %copy.61), calls=%async_computation | async-start | bytes 32768 | tf_op jit(solution)/shard_map/all_to_all | solution.py:155
  241.8 1.4 collective-permute-start.18
  243.2 1.1 collective-permute-start.20
  244.3 0.6 bitcast_dynamic-update-slice_fusion.6
  245.0 0.6 fusion.34
  245.6 0.6 bitcast_dynamic-update-slice_fusion.5
  246.3 3.8 collective-permute-done.17
  250.0 0.6 bitcast_dynamic-update-slice_fusion.4
  250.7 0.6 bitcast_dynamic-update-slice_fusion.3
  251.3 0.6 bitcast_dynamic-update-slice_fusion.2
  252.1 0.6 bitcast_dynamic-update-slice_fusion.1
  252.7 1.1 collective-permute-done.21
  253.8 0.6 bitcast_dynamic-update-slice_fusion
  254.5 4.5 %all-to-all-start.1 = ((bf16[8,4,8,1024]{3,2,0,1:T(8,128)(2,1)}), bf16[8,4,8,1024]{3,2,0,1:T(8,128)(2,1)S(1)}, u32[]{:S(2)}, u32[]{:S(2)}) async-start(bf16[8,4,8,1024]{3,2,0,1:T(8,128)(2,1)} %bitcast_dynamic-update-slice_fusion), calls=%async_computation.1 | async-start | bytes 1048576 | tf_op jit(solution)/shard_map/all_to_all | solution.py:154
  259.0 0.4 all-reduce.2.cloned.1.call-start
  259.5 6.4 %all-to-all-done.1 = bf16[8,4,8,1024]{3,2,0,1:T(8,128)(2,1)S(1)} async-done(((bf16[8,4,8,1024]{3,2,0,1:T(8,128)(2,1)}), bf16[8,4,8,1024]{3,2,0,1:T(8,128)(2,1)S(1)}, u32[]{:S(2)}, u32[]{:S(2)}) %all-to-all-start.1) | async-done | bytes 524320 | tf_op jit(solution)/shard_map/all_to_all | solution.py:154
  266.2 2.4 fusion.17
  268.6 8.3 %convolution_bitcast_fusion.2 = f32[8,128,128]{2,1,0:T(8,128)} fusion(f32[32,128,8,128]{3,1,0,2:T(8,128)S(1)} %fusion.17, bf16[32,128,128]{2,1,0:T(8,128)(2,1)S(1)} %copy-done), kind=kOutput, calls=%fused_computation.41 | convolution fusion | flops 6442450944 | bytes 18350080 | tf_op jit(solution)/shard_map/wdfa,wab->fdb/dot_general | solution.py:170
  277.0 41.5 %all-reduce.2.cloned.1.call-done = f32[8,128,128]{2,1,0:T(8,128)} async-done(((f32[8,128,128]{2,1,0:T(8,128)}), f32[8,128,128]{2,1,0:T(8,128)}) %all-reduce.2.cloned.1.call-update) | async-done | bytes 524304 | tf_op jit(solution)/shard_map/psum | solution.py:171
  318.4 2.1 conditional.5
  320.6 5.9 %copy.79 = f32[128,128,1]{1,0,2:T(8,128)} copy(f32[128,128,1]{2,1,0:T(8,128)} %bitcast.105) | data formatting | bytes 131072
  326.5 104.1 %all-gather.3.cloned.1.call-done = f32[16384,128,1]{1,0,2:T(8,128)} async-done(((f32[128,128,1]{1,0,2:T(8,128)}), f32[16384,128,1]{1,0,2:T(8,128)}) %all-gather.3.cloned.1.call-update) | async-done | bytes 8388624 | tf_op jit(solution)/shard_map/all_gather | solution.py:187
  430.6 1.7 slice_bitcast_fusion
  432.4 0.7 gather_fusion
  433.1 5.0 %select_reduce_fusion = f32[256,128]{1,0:T(8,128)S(1)} fusion(bf16[32,128,128]{2,1,0:T(8,128)(2,1)S(1)} %copy-done, pred[256,32]{0,1:T(8,128)(4,1)S(1)} %iota_compare_fusion.2, f32[256,128]{1,0:T(8,128)S(1)} %gather_fusion, pred[256]{0:T(512)(128)(4,1)S(1)} %get-tuple-element.130), kind=kOutput, calls=%fused_computation.33 | convolution fusion | flops 1612709888 | bytes 1319168 | tf_op jit(solution)/shard_map/eb,wab->ewa/dot_general | solution.py:190
  438.3 0.6 select_select_fusion
  (93 shorter events, 3.0 us)
Async XLA Ops:
  7.2 261.4 %copy-start = (bf16[32,128,128]{2,1,0:T(8,128)(2,1)S(1)}, bf16[32,128,128]{2,1,0:T(8,128)(2,1)}, u32[]{:S(2)}) copy-start(bf16[32,128,128]{2,1,0:T(8,128)(2,1)} %param.22) | copy-start | bytes 3145732
  15.2 15.4 %copy-start.10 = (s32[128,1,2,3]{0,2,3,1:T(2,128)S(1)}, s32[128,1,2,3]{0,2,3,1:T(2,128)}, u32[]{:S(2)}) copy-start(s32[128,1,2,3]{0,2,3,1:T(2,128)} %param.17) | copy-start | bytes 9220
  15.2 15.7 %copy-start.11 = (s32[8]{0:T(128)S(1)}, s32[8]{0:T(128)}, u32[]{:S(2)}) copy-start(s32[8]{0:T(128)} %constant.87.clone) | copy-start | bytes 100
  19.6 2.0 copy-start.1
  21.5 55.8 %collective-permute-start = (bf16[1,128,128]{2,1,0:T(8,128)(2,1)S(1)}, bf16[1,128,128]{2,1,0:T(8,128)(2,1)S(1)}, u32[]{:S(2)}, u32[]{:S(2)}) collective-permute-start(bf16[1,128,128]{2,1,0:T(8,128)(2,1)S(1)} %get-tuple-element.148), channel_id=1, source_target_pairs={{0,8},{8,16},{16,24},{24,32},{32,40},{40,48},{48,56},{56,64},{64,7... | collective-permute-start | bytes 98312 | tf_op jit(solution)/shard_map/ppermute | solution.py:18
  25.9 51.5 %collective-permute-start.1 = (bf16[1,128,128]{2,1,0:T(8,128)(2,1)S(1)}, bf16[1,128,128]{2,1,0:T(8,128)(2,1)S(1)}, u32[]{:S(2)}, u32[]{:S(2)}) collective-permute-start(bf16[1,128,128]{2,1,0:T(8,128)(2,1)S(1)} %get-tuple-element.149), channel_id=1, source_target_pairs={{8,0},{16,8},{24,16},{32,24},{40,32},{48,40},{56,48},{64,56},{72,6... | collective-permute-start | bytes 98312 | tf_op jit(solution)/shard_map/ppermute | solution.py:19
  28.5 48.9 %collective-permute-start.2 = (f32[128,1,128]{2,1,0:T(1,128)S(1)}, f32[128,1,128]{2,1,0:T(1,128)S(1)}, u32[]{:S(2)}, u32[]{:S(2)}) collective-permute-start(f32[128,1,128]{2,1,0:T(1,128)S(1)} %get-tuple-element.140), channel_id=1, source_target_pairs={{0,1},{1,2},{2,3},{3,4},{4,5},{5,6},{6,7},{7,0},{8,9},{9,10},{10,1... | collective-permute-start | bytes 196616 | tf_op jit(solution)/shard_map/ppermute | solution.py:18
  30.6 46.8 %collective-permute-start.3 = (f32[128,1,128]{2,1,0:T(1,128)S(1)}, f32[128,1,128]{2,1,0:T(1,128)S(1)}, u32[]{:S(2)}, u32[]{:S(2)}) collective-permute-start(f32[128,1,128]{2,1,0:T(1,128)S(1)} %get-tuple-element.141), channel_id=1, source_target_pairs={{1,0},{2,1},{3,2},{4,3},{5,4},{6,5},{7,6},{0,7},{9,8},{10,9},{11,1... | collective-permute-start | bytes 196616 | tf_op jit(solution)/shard_map/ppermute | solution.py:19
  31.4 12.8 %copy-start.3 = (s32[128,128]{1,0:T(8,128)S(1)}, s32[128,128]{1,0:T(8,128)}, u32[]{:S(2)}) copy-start(s32[128,128]{1,0:T(8,128)} %param.16) | copy-start | bytes 196612
  31.4 12.9 %collective-permute-start.8 = (s32[32]{0:T(128)S(1)}, s32[32]{0:T(128)S(1)}, u32[]{:S(2)}, u32[]{:S(2)}) collective-permute-start(s32[32]{0:T(128)S(1)} %get-tuple-element.167), channel_id=1, source_target_pairs={{0,31},{1,0},{2,1},{3,2},{4,3},{5,4},{6,5},{7,6},{8,7},{9,8},{10,9... | collective-permute-start | bytes 392 | tf_op jit(solution)/shard_map/ppermute | solution.py:27
  44.3 4.8 %collective-permute-start.9 = (s32[32]{0:T(128)S(1)}, s32[32]{0:T(128)S(1)}, u32[]{:S(2)}, u32[]{:S(2)}) collective-permute-start(s32[32]{0:T(128)S(1)} %get-tuple-element.165), channel_id=1, source_target_pairs={{0,1},{1,2},{2,3},{3,4},{4,5},{5,6},{6,7},{7,8},{8,9},{9,10},{10,1... | collective-permute-start | bytes 392 | tf_op jit(solution)/shard_map/ppermute | solution.py:27
  49.2 5.7 %collective-permute-start.10 = (s32[32]{0:T(128)S(1)}, s32[32]{0:T(128)S(1)}, u32[]{:S(2)}, u32[]{:S(2)}) collective-permute-start(s32[32]{0:T(128)S(1)} %get-tuple-element.164), channel_id=1, source_target_pairs={{0,2},{1,3},{2,4},{3,5},{4,6},{5,7},{6,8},{7,9},{8,10},{9,11},{10,... | collective-permute-start | bytes 392 | tf_op jit(solution)/shard_map/ppermute | solution.py:27
  54.9 5.1 %collective-permute-start.11 = (s32[32]{0:T(128)S(1)}, s32[32]{0:T(128)S(1)}, u32[]{:S(2)}, u32[]{:S(2)}) collective-permute-start(s32[32]{0:T(128)S(1)} %get-tuple-element.163), channel_id=1, source_target_pairs={{0,7},{1,8},{2,9},{3,10},{4,11},{5,12},{6,13},{7,14},{8,15},{9,16}... | collective-permute-start | bytes 392 | tf_op jit(solution)/shard_map/ppermute | solution.py:27
  60.0 6.0 %collective-permute-start.12 = (s32[32]{0:T(128)S(1)}, s32[32]{0:T(128)S(1)}, u32[]{:S(2)}, u32[]{:S(2)}) collective-permute-start(s32[32]{0:T(128)S(1)} %get-tuple-element.162), channel_id=1, source_target_pairs={{0,8},{1,9},{2,10},{3,11},{4,12},{5,13},{6,14},{7,15},{8,16},{9,17... | collective-permute-start | bytes 392 | tf_op jit(solution)/shard_map/ppermute | solution.py:27
  65.9 5.3 %collective-permute-start.13 = (s32[32]{0:T(128)S(1)}, s32[32]{0:T(128)S(1)}, u32[]{:S(2)}, u32[]{:S(2)}) collective-permute-start(s32[32]{0:T(128)S(1)} %get-tuple-element.161), channel_id=1, source_target_pairs={{0,9},{1,10},{2,11},{3,12},{4,13},{5,14},{6,15},{7,16},{8,17},{9,1... | collective-permute-start | bytes 392 | tf_op jit(solution)/shard_map/ppermute | solution.py:27
  71.2 6.0 %collective-permute-start.14 = (s32[32]{0:T(128)S(1)}, s32[32]{0:T(128)S(1)}, u32[]{:S(2)}, u32[]{:S(2)}) collective-permute-start(s32[32]{0:T(128)S(1)} %get-tuple-element.160), channel_id=1, source_target_pairs={{0,10},{1,11},{2,12},{3,13},{4,14},{5,15},{6,16},{7,17},{8,18},{9,... | collective-permute-start | bytes 392 | tf_op jit(solution)/shard_map/ppermute | solution.py:27
  77.4 18.3 %copy-start.5 = (f32[128,128]{1,0:T(8,128)S(1)}, f32[128,128]{1,0:T(8,128)}, u32[]{:S(2)}) copy-start(f32[128,128]{1,0:T(8,128)} %param.18) | copy-start | bytes 196612
  77.4 18.3 %copy-start.8 = (f32[128,8]{0,1:T(8,128)S(1)}, f32[128,8]{0,1:T(8,128)}, u32[]{:S(2)}) copy-start(f32[128,8]{0,1:T(8,128)} %param.20) | copy-start | bytes 12292
  134.3 11.7 %collective-permute-start.4 = (bf16[1,128,128]{2,1,0:T(8,128)(2,1)S(1)}, bf16[1,128,128]{2,1,0:T(8,128)(2,1)S(1)}, u32[]{:S(2)}, u32[]{:S(2)}) collective-permute-start(bf16[1,128,128]{2,1,0:T(8,128)(2,1)S(1)} %get-tuple-element.146), channel_id=1, source_target_pairs={{0,8},{8,16},{16,24},{24,32},{32,40},{40,48},{48,56},{56,64},{64,7... | collective-permute-start | bytes 98312 | tf_op jit(solution)/shard_map/ppermute | solution.py:18
  138.1 7.8 %collective-permute-start.5 = (bf16[1,128,128]{2,1,0:T(8,128)(2,1)S(1)}, bf16[1,128,128]{2,1,0:T(8,128)(2,1)S(1)}, u32[]{:S(2)}, u32[]{:S(2)}) collective-permute-start(bf16[1,128,128]{2,1,0:T(8,128)(2,1)S(1)} %get-tuple-element.147), channel_id=1, source_target_pairs={{8,0},{16,8},{24,16},{32,24},{40,32},{48,40},{56,48},{64,56},{72,6... | collective-permute-start | bytes 98312 | tf_op jit(solution)/shard_map/ppermute | solution.py:19
  141.4 11.4 %collective-permute-start.6 = (f32[128,1,128]{2,1,0:T(1,128)}, f32[128,1,128]{2,1,0:T(1,128)}, u32[]{:S(2)}, u32[]{:S(2)}) collective-permute-start(f32[128,1,128]{2,1,0:T(1,128)} %get-tuple-element.135), channel_id=1, source_target_pairs={{0,1},{1,2},{2,3},{3,4},{4,5},{5,6},{6,7},{7,0},{8,9},{9,10},{10,1... | collective-permute-start | bytes 196616 | tf_op jit(solution)/shard_map/ppermute | solution.py:18
  144.0 8.8 %collective-permute-start.7 = (f32[128,1,128]{2,1,0:T(1,128)}, f32[128,1,128]{2,1,0:T(1,128)}, u32[]{:S(2)}, u32[]{:S(2)}) collective-permute-start(f32[128,1,128]{2,1,0:T(1,128)} %get-tuple-element.134), channel_id=1, source_target_pairs={{1,0},{2,1},{3,2},{4,3},{5,4},{6,5},{7,6},{0,7},{9,8},{10,9},{11,1... | collective-permute-start | bytes 196616 | tf_op jit(solution)/shard_map/ppermute | solution.py:19
  165.4 4.3 copy-start.6
  228.6 14.6 %collective-permute-start.15 = (bf16[32,1024]{1,0:T(8,128)(2,1)S(1)}, bf16[32,1024]{1,0:T(8,128)(2,1)S(1)}, u32[]{:S(2)}, u32[]{:S(2)}) collective-permute-start(bf16[32,1024]{1,0:T(8,128)(2,1)S(1)} %get-tuple-element.156), channel_id=1, source_target_pairs={{0,31},{1,0},{2,1},{3,2},{4,3},{5,4},{6,5},{7,6},{8,7},{9,8},{10,9... | collective-permute-start | bytes 196616 | tf_op jit(solution)/shard_map/ppermute | solution.py:27
  232.2 22.2 %all-to-all-start = ((s32[8,4,8]{2,0,1:T(8,128)}), s32[8,4,8]{2,0,1:T(8,128)S(1)}, u32[]{:S(2)}, u32[]{:S(2)}) async-start(s32[8,4,8]{2,0,1:T(8,128)} %copy.61), calls=%async_computation | async-start | bytes 32768 | tf_op jit(solution)/shard_map/all_to_all | solution.py:155
  241.8 3.8 collective-permute-start.16
  241.8 8.3 %collective-permute-start.17 = (bf16[32,1024]{1,0:T(8,128)(2,1)S(1)}, bf16[32,1024]{1,0:T(8,128)(2,1)S(1)}, u32[]{:S(2)}, u32[]{:S(2)}) collective-permute-start(bf16[32,1024]{1,0:T(8,128)(2,1)S(1)} %get-tuple-element.154), channel_id=1, source_target_pairs={{0,2},{1,3},{2,4},{3,5},{4,6},{5,7},{6,8},{7,9},{8,10},{9,11},{10,... | collective-permute-start | bytes 196616 | tf_op jit(solution)/shard_map/ppermute | solution.py:27
  241.8 8.9 %collective-permute-start.18 = (bf16[32,1024]{1,0:T(8,128)(2,1)S(1)}, bf16[32,1024]{1,0:T(8,128)(2,1)S(1)}, u32[]{:S(2)}, u32[]{:S(2)}) collective-permute-start(bf16[32,1024]{1,0:T(8,128)(2,1)S(1)} %get-tuple-element.153), channel_id=1, source_target_pairs={{0,7},{1,8},{2,9},{3,10},{4,11},{5,12},{6,13},{7,14},{8,15},{9,16}... | collective-permute-start | bytes 196616 | tf_op jit(solution)/shard_map/ppermute | solution.py:27
  243.2 8.1 %collective-permute-start.19 = (bf16[32,1024]{1,0:T(8,128)(2,1)S(1)}, bf16[32,1024]{1,0:T(8,128)(2,1)S(1)}, u32[]{:S(2)}, u32[]{:S(2)}) collective-permute-start(bf16[32,1024]{1,0:T(8,128)(2,1)S(1)} %get-tuple-element.152), channel_id=1, source_target_pairs={{0,8},{1,9},{2,10},{3,11},{4,12},{5,13},{6,14},{7,15},{8,16},{9,17... | collective-permute-start | bytes 196616 | tf_op jit(solution)/shard_map/ppermute | solution.py:27
  243.2 8.8 %collective-permute-start.20 = (bf16[32,1024]{1,0:T(8,128)(2,1)S(1)}, bf16[32,1024]{1,0:T(8,128)(2,1)S(1)}, u32[]{:S(2)}, u32[]{:S(2)}) collective-permute-start(bf16[32,1024]{1,0:T(8,128)(2,1)S(1)} %get-tuple-element.151), channel_id=1, source_target_pairs={{0,9},{1,10},{2,11},{3,12},{4,13},{5,14},{6,15},{7,16},{8,17},{9,1... | collective-permute-start | bytes 196616 | tf_op jit(solution)/shard_map/ppermute | solution.py:27
  245.6 8.2 %collective-permute-start.21 = (bf16[32,1024]{1,0:T(8,128)(2,1)S(1)}, bf16[32,1024]{1,0:T(8,128)(2,1)S(1)}, u32[]{:S(2)}, u32[]{:S(2)}) collective-permute-start(bf16[32,1024]{1,0:T(8,128)(2,1)S(1)} %get-tuple-element.150), channel_id=1, source_target_pairs={{0,10},{1,11},{2,12},{3,13},{4,14},{5,15},{6,16},{7,17},{8,18},{9,... | collective-permute-start | bytes 196616 | tf_op jit(solution)/shard_map/ppermute | solution.py:27
  254.5 11.5 %all-to-all-start.1 = ((bf16[8,4,8,1024]{3,2,0,1:T(8,128)(2,1)}), bf16[8,4,8,1024]{3,2,0,1:T(8,128)(2,1)S(1)}, u32[]{:S(2)}, u32[]{:S(2)}) async-start(bf16[8,4,8,1024]{3,2,0,1:T(8,128)(2,1)} %bitcast_dynamic-update-slice_fusion), calls=%async_computation.1 | async-start | bytes 1048576 | tf_op jit(solution)/shard_map/all_to_all | solution.py:154
  259.0 59.4 %all-reduce.2.cloned.1.call-start = ((), (), s32[]{:S(2)}) async-start(), calls=%async_computation.2 | async-start | bytes 1048576 | tf_op jit(solution)/shard_map/psum | solution.py:171
  268.6 49.9 %copy-start.7 = (f32[128,128]{1,0:T(8,128)S(1)}, f32[128,128]{1,0:T(8,128)}, u32[]{:S(2)}) copy-start(f32[128,128]{1,0:T(8,128)} %param.19) | copy-start | bytes 196612
  268.6 49.9 %copy-start.9 = (f32[8,128]{1,0:T(8,128)S(1)}, f32[8,128]{1,0:T(8,128)}, u32[]{:S(2)}) copy-start(f32[8,128]{1,0:T(8,128)} %param.21) | copy-start | bytes 12292
  276.9 153.7 %all-gather.3.cloned.1.call-start = ((), (), s32[]{:S(2)}) async-start(), calls=%async_computation.3 | async-start | bytes 8454144 | tf_op jit(solution)/shard_map/all_gather | solution.py:187
  320.6 117.7 %copy-start.4 = (s32[128,128]{1,0:T(8,128)S(1)}, s32[128,128]{1,0:T(8,128)}, u32[]{:S(2)}) copy-start(s32[128,128]{1,0:T(8,128)} %param.16) | copy-start | bytes 196612
  326.4 111.9 %copy-start.2 = (f32[128,128,1]{1,0,2:T(8,128)S(1)}, f32[128,128,1]{1,0,2:T(8,128)}, u32[]{:S(2)}) copy-start(f32[128,128,1]{1,0,2:T(8,128)} %copy.79) | copy-start | bytes 196612
Sparse Core Ops, SparseCore 0:
  277.0 41.3 all-reduce.1
  326.6 104.0 all-gather.2
where the time goes:
time: 453 us; the launch traced here: 446 us
  waiting for transfers between devices  187 us (41%)
  matrix products  90.1 us (20%)
  local copies, waits for them, and re-layouts  62 us (14%)
  other arithmetic  47.9 us (11%)
  starting transfers between devices  42.3 us (9%)
  between operations  14.7 us (3%)
    all_gather x1, waiting for transfers between devices, local(): lax.all_gather(surface, ('comp', 'lat', 'lon'), axis=0, tiled=True)  104 us
    dot_general x2, matrix products, column_physics(): jnp.einsum('rck,kj->rcj', values, mixing, precision=HIGHEST)  55.3 us
    psum x1, waiting for transfers between devices, local(): forcing = lax.psum(partial_forcing, 'comp')  41.5 us
    ppermute x14, waiting for transfers between devices, from_behind(): return lax.ppermute(value, axis, pairs)  34.5 us
    unnamed x41, local copies, waits for them, and re-layouts  20.5 us
    dot_general x2, matrix products, advance(): jnp.einsum('rck,kf->frc', moved, flux_map, precision=HIGHEST)  18.8 us
    sub x1, other arithmetic, local(): spread = below + above + sides[:, :-2] + sides[:, 2:] - 4.0 * current  18.3 us
    slice x2, local copies, waits for them, and re-layouts, local(): current[1:]  17.7 us
  transfers between devices with their start and end apart: 26, of which 12 were waited for; matrix products, arithmetic and copies ran while one was open for 6% of the time, Pallas kernels for 0%

commit v1 on v0

--- a/solution.py
+++ b/solution.py
@@ -6,6 +6,28 @@
 SMOOTHING = 0.2
 PHYSICS = 0.5
 HIGHEST = lax.Precision.HIGHEST
+
+
+def in_blocks(x, dim, peers):
+    before, after = (x.shape[:dim], x.shape[dim + 1 :])
+    return jnp.moveaxis(x.reshape(*before, peers, -1, *after), dim, 0)
+
+
+def in_order(blocks, dim):
+    shape = list(blocks.shape[1:])
+    shape[dim] *= blocks.shape[0]
+    return jnp.moveaxis(blocks, 0, dim).reshape(shape)
+
+
+def swapped_with_each(value, axis, split_dim, concat_dim):
+    length, index = (lax.axis_size(axis), lax.axis_index(axis))
+    blocks = in_blocks(value, split_dim, length)
+    outs = [blocks[index]]
+    for hop in range(1, length):
+        sent = blocks[index ^ hop]
+        outs.append(lax.ppermute(sent, axis, [(i, i ^ hop) for i in range(length)]))
+    blocks = jnp.stack(outs)[index ^ jnp.arange(length)]
+    return in_order(blocks, concat_dim)
 
 
 def with_halo(shard, sides, width, wrap):
@@ -152,9 +174,7 @@
     stacked_labels = jnp.stack(moved_labels).reshape(neighbour_count, comp_count, quarter)
     arrived, arrived_labels = (
         lax.all_to_all(stacked_blocks, "comp", split_axis=1, concat_axis=1, tiled=True),
-        lax.all_to_all(
-            shortened(stacked_labels), "comp", split_axis=1, concat_axis=1, tiled=True
-        ).astype(stacked_labels.dtype),
+        swapped_with_each(shortened(stacked_labels), "comp", 1, 1).astype(stacked_labels.dtype),
     )
     weights_wide = regrid_weights.astype(jnp.float32)
     label_ids = jnp.arange(weight_count * tile_rows, dtype=jnp.int32)

time: 453 us -> 432 us (0.954)
  waiting for transfers between devices: 187 us -> 165 us
    ppermute x14, waiting for transfers between devices: 34.5 us -> 16.6 us  [from_behind(): return lax.ppermute(value, axis, pairs)]
    all_to_all x1 -> x0, starting transfers between devices: 9.55 us -> none  [local(): lax.all_to_all(shortened(stacked_labels), 'comp', split_axis=1, concat_ax...]
    all_to_all x1, waiting for transfers between devices: 6.4 us -> 0.01 us  [local(): lax.all_to_all(stacked_blocks, 'comp', split_axis=1, concat_axis=1, tiled...]
    ppermute x14, starting transfers between devices: 10.4 us -> 16.4 us  [from_behind(): return lax.ppermute(value, axis, pairs)]
    unnamed x41 -> x55, local copies, waits for them, and re-layouts: 20.5 us -> 20.5 us
    cond x2 -> x4, local copies, waits for them, and re-layouts: 11.2 us -> 11.2 us
  transfers between devices with their start and end apart: 26 -> 28, of which waited for: 12 -> 11; matrix products, arithmetic and copies ran while one was open for 6% -> 7% of each run, Pallas kernels for 0% -> 0%
where the time goes in v1:
time: 432 us; the launch traced here: 426 us
  waiting for transfers between devices  165 us (38%)
  matrix products  90.1 us (21%)
  local copies, waits for them, and re-layouts  63.1 us (15%)
  other arithmetic  48.5 us (11%)
  starting transfers between devices  41.8 us (10%)
  between operations  14.8 us (3%)
    all_gather x1, waiting for transfers between devices, local(): lax.all_gather(surface, ('comp', 'lat', 'lon'), axis=0, tiled=True)  104 us
    dot_general x2, matrix products, column_physics(): jnp.einsum('rck,kj->rcj', values, mixing, precision=HIGHEST)  55.4 us
    psum x1, waiting for transfers between devices, local(): forcing = lax.psum(partial_forcing, 'comp')  40.8 us
    unnamed x55, local copies, waits for them, and re-layouts  20.5 us
    dot_general x2, matrix products, advance(): jnp.einsum('rck,kf->frc', moved, flux_map, precision=HIGHEST)  18.8 us
    sub x1, other arithmetic, local(): spread = below + above + sides[:, :-2] + sides[:, 2:] - 4.0 * current  18.4 us
    slice x2, local copies, waits for them, and re-layouts, local(): current[1:]  17.7 us
    ppermute x14, waiting for transfers between devices, from_behind(): return lax.ppermute(value, axis, pairs)  16.6 us
  transfers between devices with their start and end apart: 28, of which 11 were waited for; matrix products, arithmetic and copies ran while one was open for 7% of the time, Pallas kernels for 0%

profile of v1, /device:TPU:1, one launch (start us, length us, event | category | flops | bytes accessed | tf_op | source)
XLA Modules:
  0.0 426.0 jit_solution(6878935714308280915)
XLA Ops:
  7.2 8.0 %copy.115 = f32[128,128,128]{2,1,0:T(8,128)} copy(f32[128,128,128]{2,1,0:T(8,128)} %param.15) | data formatting | bytes 16777216
  15.2 4.4 %convert_element_type.30 = bf16[128,128,128]{2,1,0:T(8,128)(2,1)S(1)} convert(f32[128,128,128]{2,1,0:T(8,128)} %copy.115) | non-fusion elementwise | flops 2097152 | bytes 12582912 | tf_op jit(solution)/shard_map/convert_element_type | solution.py:115
  19.6 2.0 copy-done.1
  21.5 4.4 %collective-permute-start = (bf16[1,128,128]{2,1,0:T(8,128)(2,1)S(1)}, bf16[1,128,128]{2,1,0:T(8,128)(2,1)S(1)}, u32[]{:S(2)}, u32[]{:S(2)}) collective-permute-start(bf16[1,128,128]{2,1,0:T(8,128)(2,1)S(1)} %get-tuple-element.148), channel_id=1, source_target_pairs={{0,8},{8,16},{16,24},{24,32},{32,40},{40,48},{48,56},{56,64},{64,7... | collective-permute-start | bytes 98312 | tf_op jit(solution)/shard_map/ppermute | solution.py:40
  25.9 1.3 collective-permute-start.1
  27.2 1.3 fusion.43
  28.5 2.1 collective-permute-start.2
  31.5 1.7 collective-permute-start.9
  33.2 10.9 %fusion.42 = (f32[127,128,128]{2,1,0:T(8,128)}, f32[127,128,128]{2,1,0:T(8,128)}) fusion(f32[128,128,128]{2,1,0:T(8,128)} %copy.115), kind=kLoop, calls=%fused_computation.112 | loop fusion | bytes 33292288 | tf_op jit(solution)/shard_map/slice | solution.py:119
  44.9 1.2 collective-permute-start.10
  46.2 1.5 collective-permute-start.11
  47.8 7.0 %collective-permute-done.10 = s32[32]{0:T(128)S(1)} collective-permute-done((s32[32]{0:T(128)S(1)}, s32[32]{0:T(128)S(1)}, u32[]{:S(2)}, u32[]{:S(2)}) %collective-permute-start.10) | collective-permute-done | bytes 160 | tf_op jit(solution)/shard_map/ppermute | solution.py:49
  55.1 3.3 collective-permute-done.12
  58.5 1.8 collective-permute-done.13
  60.3 2.5 collective-permute-start.3
  63.5 1.0 collective-permute-done.14
  64.4 0.7 stack.68
  65.2 18.4 %fusion.15 = f32[128,128,128]{2,1,0:T(8,128)} fusion(f32[128,1,128]{2,1,0:T(1,128)S(1)} %collective-permute-done.3, f32[128,128,128]{2,1,0:T(8,128)} %copy.115, f32[128,1,128]{2,1,0:T(1,128)S(1)} %collective-permute-done.2, f32[127,128,128]{2,1,0:T(8,128)} %get-tuple-element.139, f32[1,128,128]{2,1,0:T(8,128)S(1)} %get-tuple-element.145, ...), kind=kLoop, calls=%fused_computation.28 | loop fusion | flops 18874368 | bytes 33685504 | tf_op jit(solution)/shard_map/sub | solution.py:121
  83.5 27.6 %conditional.3 = (f32[128,128,128]{2,1,0:T(8,128)}, f32[8,128,128]{2,0,1:T(8,128)S(1)}) conditional(s32[]{:T(128)} %convert_element_type.29, (f32[128,128,128]{2,1,0:T(8,128)}, f32[128,128,128]{2,1,0:T(8,128)}, f32[128,128]{1,0:T(8,128)S(1)}, f32[128,8]{0,1:T(8,128)}) %tuple.90, f32[128,128,128]{2,1,0:T(8,128)} %copy.115), branch_computations={%region_0.1_spmd, %region_1.2_spmd} | conditional | flops 3435134976 | bytes 50941996 | solution.py:134
  83.7 3.4 copy.113
  87.1 14.6 %multiply_add_fusion = f32[128,128,128]{2,1,0:T(8,128)} fusion(f32[128,128,128]{2,1,0:T(8,128)S(1)} %copy.113, f32[128,128,128]{2,1,0:T(8,128)} %get-tuple-element.62, f32[128,128]{1,0:T(8,128)S(1)} %get-tuple-element.63), kind=kOutput, calls=%fused_computation.2 | convolution fusion | flops 3233808384 | bytes 25231360 | tf_op jit(solution)/shard_map/cond/branch_0_fun/rck,kj->rcj/dot_general | solution.py:57
  101.7 9.4 %convolution_bitcast_fusion = f32[8,128,128]{2,0,1:T(8,128)S(1)} fusion(f32[128,128,128]{2,1,0:T(8,128)} %multiply_add_fusion, f32[128,8]{0,1:T(8,128)S(1)} %copy-done.9), kind=kOutput, calls=%fused_computation.4 | convolution fusion | flops 201326592 | bytes 8916992 | tf_op jit(solution)/shard_map/cond/branch_0_fun/rck,kf->frc/dot_general | solution.py:129
  111.1 4.4 %convert_element_type.32 = bf16[128,128,128]{2,1,0:T(8,128)(2,1)S(1)} convert(f32[128,128,128]{2,1,0:T(8,128)} %get-tuple-element.86) | non-fusion elementwise | flops 2097152 | bytes 12582912 | tf_op jit(solution)/shard_map/convert_element_type | solution.py:115
  115.4 6.7 %fusion.41 = (f32[127,128,128]{2,1,0:T(8,128)S(1)}, f32[127,128,128]{2,1,0:T(8,128)S(1)}) fusion(f32[128,128,128]{2,1,0:T(8,128)} %get-tuple-element.86), kind=kLoop, calls=%fused_computation.111 | loop fusion | bytes 33292288 | tf_op jit(solution)/shard_map/slice | solution.py:119
  122.2 1.3 collective-permute-start.4
  123.5 1.3 collective-permute-start.5
  124.8 1.9 fusion.40
  126.8 1.7 collective-permute-start.6
  128.4 1.9 collective-permute-start.7
  130.4 6.9 %pad_maximum_fusion.4 = (f32[128,128,128]{2,1,0:T(8,128)}, f32[128,128,128]{2,1,0:T(8,128)}) fusion(f32[127,128,128]{2,1,0:T(8,128)S(1)} %get-tuple-element.137, f32[1,128,128]{2,1,0:T(8,128)S(1)} %get-tuple-element.143, f32[1,128,128]{2,1,0:T(8,128)S(1)} %get-tuple-element.142, f32[127,128,128]{2,1,0:T(8,128)S(1)} %get-tuple-element.136), kind=kLoop, calls=%fused_computation.32 | loop fusion | flops 4194304 | bytes 33554432 | tf_op jit(solution)/shard_map/concatenate | solution.py:118
  137.2 12.5 %pad_maximum_fusion.1 = (f32[128,129,128]{2,1,0:T(8,128)}, f32[128,129,128]{2,1,0:T(8,128)}) fusion(f32[128,1,128]{2,1,0:T(1,128)} %collective-permute-done.7, f32[128,128,128]{2,1,0:T(8,128)} %get-tuple-element.86, f32[128,1,128]{2,1,0:T(1,128)} %collective-permute-done.6), kind=kLoop, calls=%fused_computation.25 | loop fusion | flops 4227072 | bytes 25427968 | tf_op jit(solution)/shard_map/concatenate | solution.py:42
  149.8 4.4 %broadcast.142 = f32[128,128,128]{2,1,0:T(8,128)} broadcast(f32[]{:T(128)} %constant.80.clone.1), dimensions={} | broadcast | bytes 8388612 | tf_op jit(solution)/shard_map/broadcast.23
  154.2 58.2 %conditional.4 = ((f32[128,128,128]{2,1,0:T(8,128)}, f32[8,128,128]{2,0,1:T(8,128)S(1)})) conditional(s32[]{:T(128)} %convert_element_type.29, (f32[128,128,128]{2,1,0:T(8,128)}, f32[128,128,128]{2,1,0:T(8,128)}, f32[128,129,128]{2,1,0:T(8,128)}, f32[128,129,128]{2,1,0:T(8,128)}, f32[128,128,128]{2,1,0:T(8,128)}, ...), branch_computations={%region_2.3_spmd, %region_3.4_spmd} | conditional | flops 3456237568 | bytes 135335968 | solution.py:134
  154.4 7.8 %copy.114 = f32[128,128,128]{2,1,0:T(8,128)} copy(f32[128,128,128]{2,1,0:T(8,128)} %get-tuple-element.65) | data formatting | bytes 16777216 | tf_op jit(solution)/shard_map/cond
  162.2 40.8 %multiply_add_fusion.3 = f32[128,128,128]{2,1,0:T(8,128)} fusion(f32[128,128,128]{2,1,0:T(8,128)} %copy.114, f32[128,128,128]{2,1,0:T(8,128)} %get-tuple-element.70, f32[128,129,128]{2,1,0:T(8,128)} %get-tuple-element.69, f32[128,129,128]{2,1,0:T(8,128)} %get-tuple-element.68, f32[128,128,128]{2,1,0:T(8,128)} %get-tuple-element.66, ...), kind=kOutput, calls=%fused_computation.8 | convolution fusion | flops 3254779904 | bytes 109117440 | tf_op jit(solution)/shard_map/cond/branch_0_fun/rck,kj->rcj/dot_general | solution.py:57
  203.0 9.4 %fusion.3 = f32[8,128,128]{2,0,1:T(8,128)S(1)} fusion(f32[8,128,128]{2,0,1:T(8,128)S(1)} %get-tuple-element.72, f32[128,128,128]{2,1,0:T(8,128)} %multiply_add_fusion.3, f32[128,8]{0,1:T(8,128)S(1)} %get-tuple-element.73), kind=kOutput, calls=%fused_computation.11 | convolution fusion | flops 201457664 | bytes 9441280 | tf_op jit(solution)/shard_map/cond/branch_0_fun/rck,kf->frc/dot_general | solution.py:129
  213.0 3.0 collective-permute-start.18
  216.1 2.7 collective-permute-start.21
  218.7 1.0 collective-permute-start.22
  219.7 5.1 %collective-permute-start.23 = (bf16[32,1024]{1,0:T(8,128)(2,1)S(1)}, bf16[32,1024]{1,0:T(8,128)(2,1)S(1)}, u32[]{:S(2)}, u32[]{:S(2)}) collective-permute-start(bf16[32,1024]{1,0:T(8,128)(2,1)S(1)} %get-tuple-element.151), channel_id=1, source_target_pairs={{0,9},{1,10},{2,11},{3,12},{4,13},{5,14},{6,15},{7,16},{8,17},{9,1... | collective-permute-start | bytes 196616 | tf_op jit(solution)/shard_map/ppermute | solution.py:49
  224.8 0.6 bitcast_dynamic-update-slice_fusion.6
  226.6 2.2 collective-permute-done.20
  228.8 0.6 bitcast_dynamic-update-slice_fusion.4
  229.5 0.7 bitcast_dynamic-update-slice_fusion.3
  230.1 0.6 bitcast_dynamic-update-slice_fusion.2
  230.8 0.6 bitcast_dynamic-update-slice_fusion.1
  231.4 1.3 collective-permute-done.24
  232.7 0.6 bitcast_dynamic-update-slice_fusion
  233.4 4.5 %all-to-all-start = ((bf16[8,4,8,1024]{3,2,0,1:T(8,128)(2,1)}), bf16[8,4,8,1024]{3,2,0,1:T(8,128)(2,1)S(1)}, u32[]{:S(2)}, u32[]{:S(2)}) async-start(bf16[8,4,8,1024]{3,2,0,1:T(8,128)(2,1)} %bitcast_dynamic-update-slice_fusion), calls=%async_computation | async-start | bytes 1048576 | tf_op jit(solution)/shard_map/all_to_all | solution.py:176
  238.0 1.5 collective-permute-start.15
  239.5 2.4 collective-permute-start.16
  242.4 1.0 collective-permute-done.15
  243.4 1.5 collective-permute-done.16
  245.0 1.0 collective-permute-done.17
  246.9 2.4 fusion.17
  249.3 8.3 %convolution_bitcast_fusion.2 = f32[8,128,128]{2,1,0:T(8,128)} fusion(f32[32,128,8,128]{3,1,0,2:T(8,128)S(1)} %fusion.17, bf16[32,128,128]{2,1,0:T(8,128)(2,1)S(1)} %copy-done), kind=kOutput, calls=%fused_computation.42 | convolution fusion | flops 6442450944 | bytes 18350080 | tf_op jit(solution)/shard_map/wdfa,wab->fdb/dot_general | solution.py:190
  257.7 40.8 %all-reduce.2.cloned.1.call-done = f32[8,128,128]{2,1,0:T(8,128)} async-done(((f32[8,128,128]{2,1,0:T(8,128)}), f32[8,128,128]{2,1,0:T(8,128)}) %all-reduce.2.cloned.1.call-update) | async-done | bytes 524304 | tf_op jit(solution)/shard_map/psum | solution.py:191
  298.4 2.1 conditional.5
  300.6 5.9 %copy.77 = f32[128,128,1]{1,0,2:T(8,128)} copy(f32[128,128,1]{2,1,0:T(8,128)} %bitcast.121) | data formatting | bytes 131072
  306.5 104.1 %all-gather.3.cloned.1.call-done = f32[16384,128,1]{1,0,2:T(8,128)} async-done(((f32[128,128,1]{1,0,2:T(8,128)}), f32[16384,128,1]{1,0,2:T(8,128)}) %all-gather.3.cloned.1.call-update) | async-done | bytes 8388624 | tf_op jit(solution)/shard_map/all_gather | solution.py:207
  410.6 1.7 slice_bitcast_fusion
  412.4 0.7 gather_fusion.1
  413.1 5.0 %select_reduce_fusion = f32[256,128]{1,0:T(8,128)S(1)} fusion(bf16[32,128,128]{2,1,0:T(8,128)(2,1)S(1)} %copy-done, pred[256,32]{0,1:T(8,128)(4,1)S(1)} %iota_compare_fusion.2, f32[256,128]{1,0:T(8,128)S(1)} %gather_fusion.1, pred[256]{0:T(512)(128)(4,1)S(1)} %get-tuple-element.130), kind=kOutput, calls=%fused_computation.34 | convolution fusion | flops 1612709888 | bytes 1319168 | tf_op jit(solution)/shard_map/eb,wab->ewa/dot_general | solution.py:210
  418.3 0.6 select_select_fusion
  (117 shorter events, 6.4 us)
Async XLA Ops:
  7.2 242.1 %copy-start = (bf16[32,128,128]{2,1,0:T(8,128)(2,1)S(1)}, bf16[32,128,128]{2,1,0:T(8,128)(2,1)}, u32[]{:S(2)}) copy-start(bf16[32,128,128]{2,1,0:T(8,128)(2,1)} %param.22) | copy-start | bytes 3145732
  15.2 15.4 %copy-start.17 = (s32[128,1,2,3]{0,2,3,1:T(2,128)S(1)}, s32[128,1,2,3]{0,2,3,1:T(2,128)}, u32[]{:S(2)}) copy-start(s32[128,1,2,3]{0,2,3,1:T(2,128)} %param.17) | copy-start | bytes 9220
  15.2 15.7 %copy-start.19 = (s32[8]{0:T(128)S(1)}, s32[8]{0:T(128)}, u32[]{:S(2)}) copy-start(s32[8]{0:T(128)} %constant.91.clone) | copy-start | bytes 100
  19.6 2.0 copy-start.1
  21.5 43.6 %collective-permute-start = (bf16[1,128,128]{2,1,0:T(8,128)(2,1)S(1)}, bf16[1,128,128]{2,1,0:T(8,128)(2,1)S(1)}, u32[]{:S(2)}, u32[]{:S(2)}) collective-permute-start(bf16[1,128,128]{2,1,0:T(8,128)(2,1)S(1)} %get-tuple-element.148), channel_id=1, source_target_pairs={{0,8},{8,16},{16,24},{24,32},{32,40},{40,48},{48,56},{56,64},{64,7... | collective-permute-start | bytes 98312 | tf_op jit(solution)/shard_map/ppermute | solution.py:40
  25.9 39.2 %collective-permute-start.1 = (bf16[1,128,128]{2,1,0:T(8,128)(2,1)S(1)}, bf16[1,128,128]{2,1,0:T(8,128)(2,1)S(1)}, u32[]{:S(2)}, u32[]{:S(2)}) collective-permute-start(bf16[1,128,128]{2,1,0:T(8,128)(2,1)S(1)} %get-tuple-element.149), channel_id=1, source_target_pairs={{8,0},{16,8},{24,16},{32,24},{40,32},{48,40},{56,48},{64,56},{72,6... | collective-permute-start | bytes 98312 | tf_op jit(solution)/shard_map/ppermute | solution.py:41
  28.5 36.6 %collective-permute-start.2 = (f32[128,1,128]{2,1,0:T(1,128)S(1)}, f32[128,1,128]{2,1,0:T(1,128)S(1)}, u32[]{:S(2)}, u32[]{:S(2)}) collective-permute-start(f32[128,1,128]{2,1,0:T(1,128)S(1)} %get-tuple-element.140), channel_id=1, source_target_pairs={{0,1},{1,2},{2,3},{3,4},{4,5},{5,6},{6,7},{7,0},{8,9},{9,10},{10,1... | collective-permute-start | bytes 196616 | tf_op jit(solution)/shard_map/ppermute | solution.py:40
  30.9 13.2 %copy-start.12 = (s32[256,1]{0,1:T(1,128)}, s32[256,1]{0,1:T(1,128)S(1)}, u32[]{:S(2)}) copy-start(s32[256,1]{0,1:T(1,128)S(1)} %get-tuple-element.161) | copy-start | bytes 3076
  31.2 12.9 %copy-start.10 = (s32[256]{0:T(256)}, s32[256]{0:T(256)S(1)}, u32[]{:S(2)}) copy-start(s32[256]{0:T(256)S(1)} %get-tuple-element.175) | copy-start | bytes 3076
  31.4 13.4 %collective-permute-start.8 = (s32[32]{0:T(128)S(1)}, s32[32]{0:T(128)S(1)}, u32[]{:S(2)}, u32[]{:S(2)}) collective-permute-start(s32[32]{0:T(128)S(1)} %get-tuple-element.171), channel_id=1, source_target_pairs={{0,31},{1,0},{2,1},{3,2},{4,3},{5,4},{6,5},{7,6},{8,7},{9,8},{10,9... | collective-permute-start | bytes 392 | tf_op jit(solution)/shard_map/ppermute | solution.py:49
  31.4 13.3 %copy-start.3 = (s32[128,128]{1,0:T(8,128)S(1)}, s32[128,128]{1,0:T(8,128)}, u32[]{:S(2)}) copy-start(s32[128,128]{1,0:T(8,128)} %param.16) | copy-start | bytes 196612
  31.5 14.8 %collective-permute-start.9 = (s32[32]{0:T(128)S(1)}, s32[32]{0:T(128)S(1)}, u32[]{:S(2)}, u32[]{:S(2)}) collective-permute-start(s32[32]{0:T(128)S(1)} %get-tuple-element.169), channel_id=1, source_target_pairs={{0,1},{1,2},{2,3},{3,4},{4,5},{5,6},{6,7},{7,8},{8,9},{9,10},{10,1... | collective-permute-start | bytes 392 | tf_op jit(solution)/shard_map/ppermute | solution.py:49
  44.9 10.0 %collective-permute-start.10 = (s32[32]{0:T(128)S(1)}, s32[32]{0:T(128)S(1)}, u32[]{:S(2)}, u32[]{:S(2)}) collective-permute-start(s32[32]{0:T(128)S(1)} %get-tuple-element.168), channel_id=1, source_target_pairs={{0,2},{1,3},{2,4},{3,5},{4,6},{5,7},{6,8},{7,9},{8,10},{9,11},{10,... | collective-permute-start | bytes 392 | tf_op jit(solution)/shard_map/ppermute | solution.py:49
  46.2 8.7 %collective-permute-start.11 = (s32[32]{0:T(128)S(1)}, s32[32]{0:T(128)S(1)}, u32[]{:S(2)}, u32[]{:S(2)}) collective-permute-start(s32[32]{0:T(128)S(1)} %get-tuple-element.167), channel_id=1, source_target_pairs={{0,7},{1,8},{2,9},{3,10},{4,11},{5,12},{6,13},{7,14},{8,15},{9,16}... | collective-permute-start | bytes 392 | tf_op jit(solution)/shard_map/ppermute | solution.py:49
  54.8 3.6 collective-permute-start.12
  54.9 5.4 %collective-permute-start.13 = (s32[32]{0:T(128)S(1)}, s32[32]{0:T(128)S(1)}, u32[]{:S(2)}, u32[]{:S(2)}) collective-permute-start(s32[32]{0:T(128)S(1)} %get-tuple-element.165), channel_id=1, source_target_pairs={{0,9},{1,10},{2,11},{3,12},{4,13},{5,14},{6,15},{7,16},{8,17},{9,1... | collective-permute-start | bytes 392 | tf_op jit(solution)/shard_map/ppermute | solution.py:49
  58.4 6.0 %collective-permute-start.14 = (s32[32]{0:T(128)S(1)}, s32[32]{0:T(128)S(1)}, u32[]{:S(2)}, u32[]{:S(2)}) collective-permute-start(s32[32]{0:T(128)S(1)} %get-tuple-element.164), channel_id=1, source_target_pairs={{0,10},{1,11},{2,12},{3,13},{4,14},{5,15},{6,16},{7,17},{8,18},{9,... | collective-permute-start | bytes 392 | tf_op jit(solution)/shard_map/ppermute | solution.py:49
  60.3 4.8 %collective-permute-start.3 = (f32[128,1,128]{2,1,0:T(1,128)S(1)}, f32[128,1,128]{2,1,0:T(1,128)S(1)}, u32[]{:S(2)}, u32[]{:S(2)}) collective-permute-start(f32[128,1,128]{2,1,0:T(1,128)S(1)} %get-tuple-element.141), channel_id=1, source_target_pairs={{1,0},{2,1},{3,2},{4,3},{5,4},{6,5},{7,6},{0,7},{9,8},{10,9},{11,1... | collective-permute-start | bytes 196616 | tf_op jit(solution)/shard_map/ppermute | solution.py:41
  65.1 18.4 %copy-start.5 = (f32[128,128]{1,0:T(8,128)S(1)}, f32[128,128]{1,0:T(8,128)}, u32[]{:S(2)}) copy-start(f32[128,128]{1,0:T(8,128)} %param.18) | copy-start | bytes 196612
  87.1 14.6 %copy-start.9 = (f32[128,8]{0,1:T(8,128)S(1)}, f32[128,8]{0,1:T(8,128)}, u32[]{:S(2)}) copy-start(f32[128,8]{0,1:T(8,128)} %get-tuple-element.64) | copy-start | bytes 12292 | tf_op jit(solution)/shard_map/cond
  122.2 8.1 %collective-permute-start.4 = (bf16[1,128,128]{2,1,0:T(8,128)(2,1)S(1)}, bf16[1,128,128]{2,1,0:T(8,128)(2,1)S(1)}, u32[]{:S(2)}, u32[]{:S(2)}) collective-permute-start(bf16[1,128,128]{2,1,0:T(8,128)(2,1)S(1)} %get-tuple-element.146), channel_id=1, source_target_pairs={{0,8},{8,16},{16,24},{24,32},{32,40},{40,48},{48,56},{56,64},{64,7... | collective-permute-start | bytes 98312 | tf_op jit(solution)/shard_map/ppermute | solution.py:40
  123.5 6.8 %collective-permute-start.5 = (bf16[1,128,128]{2,1,0:T(8,128)(2,1)S(1)}, bf16[1,128,128]{2,1,0:T(8,128)(2,1)S(1)}, u32[]{:S(2)}, u32[]{:S(2)}) collective-permute-start(bf16[1,128,128]{2,1,0:T(8,128)(2,1)S(1)} %get-tuple-element.147), channel_id=1, source_target_pairs={{8,0},{16,8},{24,16},{32,24},{40,32},{48,40},{56,48},{64,56},{72,6... | collective-permute-start | bytes 98312 | tf_op jit(solution)/shard_map/ppermute | solution.py:41
  126.8 10.5 %collective-permute-start.6 = (f32[128,1,128]{2,1,0:T(1,128)}, f32[128,1,128]{2,1,0:T(1,128)}, u32[]{:S(2)}, u32[]{:S(2)}) collective-permute-start(f32[128,1,128]{2,1,0:T(1,128)} %get-tuple-element.135), channel_id=1, source_target_pairs={{0,1},{1,2},{2,3},{3,4},{4,5},{5,6},{6,7},{7,0},{8,9},{9,10},{10,1... | collective-permute-start | bytes 196616 | tf_op jit(solution)/shard_map/ppermute | solution.py:40
  128.4 8.8 %collective-permute-start.7 = (f32[128,1,128]{2,1,0:T(1,128)}, f32[128,1,128]{2,1,0:T(1,128)}, u32[]{:S(2)}, u32[]{:S(2)}) collective-permute-start(f32[128,1,128]{2,1,0:T(1,128)} %get-tuple-element.134), channel_id=1, source_target_pairs={{1,0},{2,1},{3,2},{4,3},{5,4},{6,5},{7,6},{0,7},{9,8},{10,9},{11,1... | collective-permute-start | bytes 196616 | tf_op jit(solution)/shard_map/ppermute | solution.py:41
  149.8 4.4 %copy-start.6 = (f32[128,128]{1,0:T(8,128)S(1)}, f32[128,128]{1,0:T(8,128)}, u32[]{:S(2)}) copy-start(f32[128,128]{1,0:T(8,128)} %param.18) | copy-start | bytes 196612
  149.8 4.4 %copy-start.8 = (f32[128,8]{0,1:T(8,128)S(1)}, f32[128,8]{0,1:T(8,128)}, u32[]{:S(2)}) copy-start(f32[128,8]{0,1:T(8,128)} %param.20) | copy-start | bytes 12292
  154.1 58.4 %copy-start.11 = (s32[256]{0:T(256)S(1)}, s32[256]{0:T(256)}, u32[]{:S(2)}) copy-start(s32[256]{0:T(256)} %copy-done.10) | copy-start | bytes 3076
  154.1 61.8 %copy-start.15 = (s32[1,4,1,8]{3,1,2,0:T(4,128)S(1)}, s32[1,4,1,8]{3,1,2,0:T(4,128)}, u32[]{:S(2)}) copy-start(s32[1,4,1,8]{3,1,2,0:T(4,128)} %stack.67) | copy-start | bytes 388
  154.1 83.8 %copy-start.14 = (s32[1,4,1,8]{3,1,2,0:T(4,128)S(1)}, s32[1,4,1,8]{3,1,2,0:T(4,128)}, u32[]{:S(2)}) copy-start(s32[1,4,1,8]{3,1,2,0:T(4,128)} %stack.68) | copy-start | bytes 388
  154.1 88.2 %copy-start.18 = (s32[4]{0:T(128)S(1)}, s32[4]{0:T(128)}, u32[]{:S(2)}) copy-start(s32[4]{0:T(128)} %fusion.38) | copy-start | bytes 52
  213.0 6.8 %collective-permute-start.18 = (bf16[32,1024]{1,0:T(8,128)(2,1)S(1)}, bf16[32,1024]{1,0:T(8,128)(2,1)S(1)}, u32[]{:S(2)}, u32[]{:S(2)}) collective-permute-start(bf16[32,1024]{1,0:T(8,128)(2,1)S(1)} %get-tuple-element.156), channel_id=1, source_target_pairs={{0,31},{1,0},{2,1},{3,2},{4,3},{5,4},{6,5},{7,6},{8,7},{9,8},{10,9... | collective-permute-start | bytes 196616 | tf_op jit(solution)/shard_map/ppermute | solution.py:49
  216.0 10.0 %collective-permute-start.19 = (bf16[32,1024]{1,0:T(8,128)(2,1)S(1)}, bf16[32,1024]{1,0:T(8,128)(2,1)S(1)}, u32[]{:S(2)}, u32[]{:S(2)}) collective-permute-start(bf16[32,1024]{1,0:T(8,128)(2,1)S(1)} %get-tuple-element.155), channel_id=1, source_target_pairs={{0,1},{1,2},{2,3},{3,4},{4,5},{5,6},{6,7},{7,8},{8,9},{9,10},{10,1... | collective-permute-start | bytes 196616 | tf_op jit(solution)/shard_map/ppermute | solution.py:49
  216.0 12.9 %collective-permute-start.20 = (bf16[32,1024]{1,0:T(8,128)(2,1)S(1)}, bf16[32,1024]{1,0:T(8,128)(2,1)S(1)}, u32[]{:S(2)}, u32[]{:S(2)}) collective-permute-start(bf16[32,1024]{1,0:T(8,128)(2,1)S(1)} %get-tuple-element.154), channel_id=1, source_target_pairs={{0,2},{1,3},{2,4},{3,5},{4,6},{5,7},{6,8},{7,9},{8,10},{9,11},{10,... | collective-permute-start | bytes 196616 | tf_op jit(solution)/shard_map/ppermute | solution.py:49
  216.1 13.4 %collective-permute-start.21 = (bf16[32,1024]{1,0:T(8,128)(2,1)S(1)}, bf16[32,1024]{1,0:T(8,128)(2,1)S(1)}, u32[]{:S(2)}, u32[]{:S(2)}) collective-permute-start(bf16[32,1024]{1,0:T(8,128)(2,1)S(1)} %get-tuple-element.153), channel_id=1, source_target_pairs={{0,7},{1,8},{2,9},{3,10},{4,11},{5,12},{6,13},{7,14},{8,15},{9,16}... | collective-permute-start | bytes 196616 | tf_op jit(solution)/shard_map/ppermute | solution.py:49
  218.7 11.4 %collective-permute-start.22 = (bf16[32,1024]{1,0:T(8,128)(2,1)S(1)}, bf16[32,1024]{1,0:T(8,128)(2,1)S(1)}, u32[]{:S(2)}, u32[]{:S(2)}) collective-permute-start(bf16[32,1024]{1,0:T(8,128)(2,1)S(1)} %get-tuple-element.152), channel_id=1, source_target_pairs={{0,8},{1,9},{2,10},{3,11},{4,12},{5,13},{6,14},{7,15},{8,16},{9,17... | collective-permute-start | bytes 196616 | tf_op jit(solution)/shard_map/ppermute | solution.py:49
  219.7 11.1 %collective-permute-start.23 = (bf16[32,1024]{1,0:T(8,128)(2,1)S(1)}, bf16[32,1024]{1,0:T(8,128)(2,1)S(1)}, u32[]{:S(2)}, u32[]{:S(2)}) collective-permute-start(bf16[32,1024]{1,0:T(8,128)(2,1)S(1)} %get-tuple-element.151), channel_id=1, source_target_pairs={{0,9},{1,10},{2,11},{3,12},{4,13},{5,14},{6,15},{7,16},{8,17},{9,1... | collective-permute-start | bytes 196616 | tf_op jit(solution)/shard_map/ppermute | solution.py:49
  226.0 6.7 %collective-permute-start.24 = (bf16[32,1024]{1,0:T(8,128)(2,1)S(1)}, bf16[32,1024]{1,0:T(8,128)(2,1)S(1)}, u32[]{:S(2)}, u32[]{:S(2)}) collective-permute-start(bf16[32,1024]{1,0:T(8,128)(2,1)S(1)} %get-tuple-element.150), channel_id=1, source_target_pairs={{0,10},{1,11},{2,12},{3,13},{4,14},{5,15},{6,16},{7,17},{8,18},{9,... | collective-permute-start | bytes 196616 | tf_op jit(solution)/shard_map/ppermute | solution.py:49
  233.4 13.2 %all-to-all-start = ((bf16[8,4,8,1024]{3,2,0,1:T(8,128)(2,1)}), bf16[8,4,8,1024]{3,2,0,1:T(8,128)(2,1)S(1)}, u32[]{:S(2)}, u32[]{:S(2)}) async-start(bf16[8,4,8,1024]{3,2,0,1:T(8,128)(2,1)} %bitcast_dynamic-update-slice_fusion), calls=%async_computation | async-start | bytes 1048576 | tf_op jit(solution)/shard_map/all_to_all | solution.py:176
  237.9 60.5 %all-reduce.2.cloned.1.call-start = ((), (), s32[]{:S(2)}) async-start(), calls=%async_computation.1 | async-start | bytes 1048576 | tf_op jit(solution)/shard_map/psum | solution.py:191
  238.0 5.4 %collective-permute-start.15 = (s32[8,1,8]{2,0,1:T(8,128)S(1)}, s32[8,1,8]{2,0,1:T(8,128)S(1)}, u32[]{:S(2)}, u32[]{:S(2)}) collective-permute-start(s32[8,1,8]{2,0,1:T(8,128)S(1)} %bitcast.132), channel_id=1, source_target_pairs={{0,32},{32,0},{64,96},{96,64},{1,33},{33,1},{65,97},{97,65},{2,34}... | collective-permute-start | bytes 776 | tf_op jit(solution)/shard_map/ppermute | solution.py:28
  239.5 5.4 %collective-permute-start.16 = (s32[8,1,8]{2,0,1:T(8,128)S(1)}, s32[8,1,8]{2,0,1:T(8,128)S(1)}, u32[]{:S(2)}, u32[]{:S(2)}) collective-permute-start(s32[8,1,8]{2,0,1:T(8,128)S(1)} %bitcast.131), channel_id=1, source_target_pairs={{0,64},{32,96},{64,0},{96,32},{1,65},{33,97},{65,1},{97,33},{2,66}... | collective-permute-start | bytes 776 | tf_op jit(solution)/shard_map/ppermute | solution.py:28
  241.9 4.1 collective-permute-start.17
  249.3 49.1 %copy-start.7 = (f32[128,128]{1,0:T(8,128)S(1)}, f32[128,128]{1,0:T(8,128)}, u32[]{:S(2)}) copy-start(f32[128,128]{1,0:T(8,128)} %param.19) | copy-start | bytes 196612
  249.3 49.1 %copy-start.16 = (f32[8,128]{1,0:T(8,128)S(1)}, f32[8,128]{1,0:T(8,128)}, u32[]{:S(2)}) copy-start(f32[8,128]{1,0:T(8,128)} %param.21) | copy-start | bytes 12292
  257.6 153.0 %all-gather.3.cloned.1.call-start = ((), (), s32[]{:S(2)}) async-start(), calls=%async_computation.2 | async-start | bytes 8454144 | tf_op jit(solution)/shard_map/all_gather | solution.py:207
  300.6 5.9 %copy-start.13 = (s32[256,1]{0,1:T(1,128)S(1)}, s32[256,1]{0,1:T(1,128)}, u32[]{:S(2)}) copy-start(s32[256,1]{0,1:T(1,128)} %copy-done.12) | copy-start | bytes 3076
  300.6 117.7 %copy-start.4 = (s32[128,128]{1,0:T(8,128)S(1)}, s32[128,128]{1,0:T(8,128)}, u32[]{:S(2)}) copy-start(s32[128,128]{1,0:T(8,128)} %param.16) | copy-start | bytes 196612
  306.4 111.8 %copy-start.2 = (f32[128,128,1]{1,0,2:T(8,128)S(1)}, f32[128,128,1]{1,0,2:T(8,128)}, u32[]{:S(2)}) copy-start(f32[128,128,1]{1,0,2:T(8,128)} %copy.77) | copy-start | bytes 196612
Sparse Core Ops, SparseCore 0:
  257.7 40.6 all-reduce.1
  306.6 104.0 all-gather.2
